TPU v7x, 256 devices: a whole 4x4x8 slice. The times are simulated.
256 devices in a mesh: band: 8 (over x, core), grid: 32 (over z, y).
Axes of the slice: x: 4, y: 4, z: 8, core: 2. Of those that a mesh axis runs over, the one named last changes fastest.
Arguments:
- coeffs: float32 [2, 8, 22016, 128], P(None, 'band', 'grid'), may hold values from -6 to 6
- stick_ids: int32 [22016], replicated, may hold values from -1 to 16383, as said below
- band_weights: float32 [8], P('band'), may hold values from 0.02 to 0.2
- aug_functions: float32 [128, 16, 256], replicated, may hold values from -0.1875 to 0.1875
- atom_offsets: int32 [64, 3], replicated, may hold values from 0 to 255, as said below
- intersection_list: int32 [32, 7], P('grid'), may hold values from 0 to 63, as said below
- atom_slots: int32 [128], replicated, may hold values from -1 to 63, as said below
Outputs:
- density: float32 [256, 256, 256], P('grid', 'band')
- atom_totals: float32 [128, 128, 128], P('grid')
Inputs may be any that keep to these rules, and one draw needn't show every extreme that they name: `stick_ids`: every column of the 128 x 128 wave-vector columns stands in exactly one slot; empty slots hold -1; some index of grid has all its 688 slots filled. `atom_slots`: every atom stands in exactly one slot; empty slots hold -1; some index of grid has all its 4 slots filled. `atom_offsets`: columns are x0, y0, z0; atom a has z0 in a * 4 .. (a + 1) * 4 - 1. `intersection_list`: row d names 7 distinct atoms, among them every atom whose box has a layer on the planes of index d of grid.
All inputs are finite; a program needn't handle non-finite values.
Results may differ from a plain program's by a relative error of at most 0.0003.
Values sent between devices are 32-bit elements; how exact they have to be, the bound alone decides.
A program may use at most 192 MiB of HBM per device.

v0:
```python
import jax
import jax.numpy as jnp
from jax import lax
from jax.sharding import PartitionSpec as P

GRID = 256
KG = 128
BOX = 16
NFUNC = 128
HIGH = lax.Precision.HIGHEST


def dft_tables(amount, length):
    frequency = jnp.arange(amount, dtype=jnp.int32) - amount // 2
    points = jnp.arange(length, dtype=jnp.int32)
    phases = frequency[:, None] * points[None, :] % length
    angles = phases.astype(jnp.float32) * (2.0 * jnp.pi / length)
    factor = amount ** (-0.5)
    return (jnp.cos(angles) * factor, jnp.sin(angles) * factor)


def complex_apply(form, real_part, imag_part, cosine, sine):
    real_out = jnp.einsum(form, real_part, cosine, precision=HIGH) - jnp.einsum(
        form, imag_part, sine, precision=HIGH
    )
    imag_out = jnp.einsum(form, real_part, sine, precision=HIGH) + jnp.einsum(
        form, imag_part, cosine, precision=HIGH
    )
    return (real_out, imag_out)


def column_slots(stick_ids):
    total = KG * KG
    target = jnp.where(stick_ids >= 0, stick_ids, total)
    filled = (
        jnp.zeros((total + 1,), jnp.int32)
        .at[target]
        .set(jnp.arange(stick_ids.shape[0], dtype=jnp.int32))
    )
    return filled[:total]


def layer_pick(first, lowest, layers, planes):
    planes_here = first + jnp.arange(planes, dtype=jnp.int32)
    depth = (planes_here - lowest) % GRID
    return (depth[:, None] == layers[None, :]).astype(jnp.float32)


def wrap_pad(field):
    field = jnp.concatenate([field, field[..., :BOX, :]], axis=-2)
    return jnp.concatenate([field, field[..., :BOX]], axis=-1)


def fold_pad(padded):
    rows = padded[:, :GRID, :] + jnp.pad(padded[:, GRID:, :], ((0, 0), (0, GRID - BOX), (0, 0)))
    return rows[:, :, :GRID] + jnp.pad(rows[:, :, GRID:], ((0, 0), (0, 0), (0, GRID - BOX)))


def on_device(
    coeffs, stick_ids, band_weights, aug_functions, atom_offsets, intersection_list, atom_slots
):
    planes = GRID // lax.axis_size("grid")
    first_plane = lax.axis_index("grid") * planes
    listed = intersection_list[0]
    listed_offsets = atom_offsets[listed]
    listed_count = listed.shape[0]
    own_rows = atom_slots.shape[0] // lax.axis_size("grid")
    every_layer = jnp.arange(BOX, dtype=jnp.int32)
    cosine, sine = dft_tables(KG, GRID)
    slot_map = column_slots(stick_ids)
    z_real, z_imag = complex_apply("bsg,gn->bns", coeffs[0], coeffs[1], cosine, sine)
    sticks = jnp.stack([z_real, z_imag])

    def project_atom(padded_wave, offsets):
        bands_here = padded_wave.shape[1]
        pick = layer_pick(first_plane, offsets[2], every_layer, planes)
        chosen = jnp.einsum("pk,ikc->ipc", pick, aug_functions, precision=HIGH)
        window = lax.dynamic_slice(
            padded_wave, (0, 0, 0, offsets[0], offsets[1]), (2, bands_here, planes, BOX, BOX)
        )
        window = window.reshape(2, bands_here, planes, BOX * BOX)
        return jnp.einsum("ipc,xbpc->bxi", chosen, window, precision=HIGH)

    received = lax.all_to_all(sticks, "grid", split_axis=2, concat_axis=3, tiled=True)
    bands_here = received.shape[1]
    spectra = received[:, :, :, slot_map].reshape(2, bands_here, planes, KG, KG)
    y_real, y_imag = complex_apply("bpxy,yn->bpxn", spectra[0], spectra[1], cosine, sine)
    x_real, x_imag = complex_apply("bpxn,xm->bpmn", y_real, y_imag, cosine, sine)
    band_density = x_real * x_real + x_imag * x_imag
    padded_wave = wrap_pad(jnp.stack([x_real, x_imag]))
    found = jax.vmap(lambda offsets: project_atom(padded_wave, offsets), out_axes=1)(listed_offsets)
    density = jnp.einsum("b,bpxy->pxy", band_weights, band_density, precision=HIGH)
    flat_found = jnp.transpose(found, (1, 0, 2, 3)).reshape(listed_count, -1)
    pick = (atom_slots[:, None] == listed[None, :]).astype(jnp.float32)
    owned = lax.psum_scatter(
        jnp.dot(pick, flat_found, precision=HIGH), "grid", scatter_dimension=0, tiled=True
    )
    owned = owned.reshape(own_rows, band_weights.shape[0], 2, NFUNC)
    partial_matrices = jnp.einsum("b,sbxi,sbxj->sij", band_weights, owned, owned, precision=HIGH)
    atom_totals = lax.psum(partial_matrices, "band")
    slot_pick = (listed[:, None] == atom_slots[None, :]).astype(jnp.float32)
    thickness = BOX // lax.axis_size("band")
    band_layers = lax.axis_index("band") * thickness + jnp.arange(thickness, dtype=jnp.int32)
    layers_here = lax.dynamic_slice_in_dim(
        aug_functions, lax.axis_index("band") * thickness, thickness, 1
    )
    layers_here = layers_here.reshape(NFUNC, thickness * BOX * BOX)
    halfway = jnp.einsum("sij,jc->sic", atom_totals, layers_here, precision=HIGH)
    box_part = jnp.sum(halfway * layers_here[None], axis=1)
    every_box = lax.all_gather(box_part, "grid", axis=0, tiled=True)
    mine = jnp.dot(slot_pick, every_box, precision=HIGH).reshape(listed_count, thickness, BOX * BOX)

    def box_piece(offsets, box_rows):
        pick = layer_pick(first_plane, offsets[2], band_layers, planes)
        return jnp.dot(pick, box_rows, precision=HIGH).reshape(planes, BOX, BOX)

    pieces = jax.vmap(box_piece)(listed_offsets, mine)

    def place(index, acc):
        corner = (0, listed_offsets[index, 0], listed_offsets[index, 1])
        current = lax.dynamic_slice(acc, corner, (planes, BOX, BOX))
        return lax.dynamic_update_slice(acc, current + pieces[index], corner)

    padded = lax.fori_loop(
        0, listed_count, place, jnp.zeros((planes, GRID + BOX, GRID + BOX), jnp.float32)
    )
    total = density + fold_pad(padded)
    result = lax.psum_scatter(total, "band", scatter_dimension=1, tiled=True)
    return (result, atom_totals)


def solution(mesh):
    placed = (P(None, "band", "grid", None), P(), P("band"), P(), P(), P("grid", None), P())
    return jax.shard_map(
        on_device,
        mesh=mesh,
        in_specs=placed,
        out_specs=(P("grid", "band", None), P("grid", None, None)),
        check_vma=False,
    )
```

profile of v0, /device:TPU:8, one launch (start us, length us, event | category | flops | bytes accessed | tf_op | source)
XLA Modules:
  0.0 786.7 jit_solution(15550919658142856036)
XLA Ops:
  7.2 2.4 fusion.16
  9.6 2.2 fusion.18
  11.8 2.2 fusion.8
  14.0 1.2 fusion.9
  15.4 3.0 copy.39
  18.4 11.9 %all-to-all-start = ((f32[2,1,256,688]{3,1,0,2:T(1,128)}), f32[2,1,256,688]{3,1,0,2:T(1,128)}, u32[]{:S(2)}, u32[]{:S(2)}) async-start(f32[2,1,256,688]{3,1,0,2:T(1,128)} %copy.39), calls=%async_computation | async-start | bytes 3145728 | tf_op jit(solution)/shard_map/all_to_all | solution.py:84
  31.3 81.4 %scatter_custom_fusion = s32[16385]{0:T(1024)S(1)} fusion(s32[22016]{0:T(1024)S(1)} %compare_select_fusion, s32[22016]{0:T(1024)S(1)} %iota.50, s32[]{:T(128)} %constant.80.clone.1), kind=kCustom, calls=%fused_computation.75 | custom fusion | bytes 65544 | tf_op jit(solution)/shard_map/scatter | solution.py:38
  113.0 5.2 convolution_bitcast_fusion
  118.2 2.7 copy.87
  120.9 21.8 %copy.67 = f32[2,1,8,32,688]{2,0,4,3,1:T(2,128)} copy(f32[2,1,8,32,688]{4,2,3,0,1:T(8,128)} %bitcast.131) | data formatting | bytes 2818048 | tf_op jit(solution)/shard_map/all_to_all | solution.py:84
  142.7 118.9 %gather_fusion = f32[16384,2,8]{2,1,0:T(2,128)} fusion(f32[2,8,22016]{1,0,2:T(2,128)} %bitcast.129, s32[16384]{0:T(1024)S(1)} %fusion.42), kind=kCustom, calls=%fused_computation | custom fusion | bytes 2162688 | tf_op jit(solution)/shard_map/gather | solution.py:86
  261.6 19.3 %fusion.133 = (f32[1,8,16384]{1,0,2:T(1,128)}, f32[1,8,16384]{1,0,2:T(1,128)}) fusion(f32[2,8,16384]{1,0,2:T(2,128)} %bitcast.130), kind=kLoop, calls=%fused_computation.178 | loop fusion | bytes 2097152 | tf_op jit(solution)/shard_map/slice | solution.py:87
  280.9 5.1 copy.68
  286.1 2.5 fusion.34
  288.6 2.4 fusion.27
  291.0 5.3 copy.70
  296.3 2.7 convolution_subtract_fusion.1
  299.1 2.3 fusion.37
  301.4 2.3 fusion.29
  303.7 1.5 convolution_add_fusion.1
  305.1 2.3 convolution_subtract_fusion
  307.5 2.3 convolution_add_fusion
  309.9 1.3 copy-done.3
  311.2 3.0 fusion.2
  314.1 75.1 %copy.53 = f32[2,1,8,272,272]{2,0,1,4,3:T(2,128)} copy(f32[2,1,8,272,272]{4,3,2,1,0:T(8,128)} %fusion.2) | data formatting | bytes 9469952 | tf_op jit(solution)/shard_map/concatenate | solution.py:51
  389.2 5.3 gather_fusion.2
  394.5 2.6 copy.54
  397.2 9.8 %fusion.11 = f32[1,7,2,128]{3,2,1,0:T(2,128)S(1)} fusion(f32[7,2,8,256]{3,1,2,0:T(2,128)S(1)} %copy.54, f32[7,128,8,256]{3,2,1,0:T(8,128)} %convolution_bitcast_fusion), kind=kOutput, calls=%fused_computation.34 | convolution fusion | flops 44040192 | bytes 7461888 | tf_op jit(solution)/shard_map/vmap(ipc,xbpc->bxi)/dot_general | solution.py:82
  409.9 141.7 %all-reduce.8.cloned.1.call-done = f32[128,256]{1,0:T(8,128)} async-done(((f32[128,256]{1,0:T(8,128)}), f32[128,256]{1,0:T(8,128)}) %all-reduce.8.cloned.1.call-update) | async-done | bytes 131088
  552.3 1.3 fusion.56
  554.2 64.0 %all-reduce.6.cloned.1.call-done = f32[4,128,128]{2,1,0:T(8,128)} async-done(((f32[4,128,128]{2,1,0:T(8,128)}), f32[4,128,128]{2,1,0:T(8,128)}) %all-reduce.6.cloned.1.call-update) | async-done | bytes 262160 | tf_op jit(solution)/shard_map/psum | solution.py:100
  618.2 2.0 fusion.10
  620.1 49.4 %all-gather = f32[32,4,512]{2,1,0:T(4,128)S(1)} all-gather(f32[1,4,512]{2,1,0:T(4,128)S(1)} %bitcast.135), channel_id=1, replica_groups=mesh['band'=8,'grid'=32] {'grid'}, dimensions={0}, use_global_device_ids=true | all-gather | bytes 270336 | tf_op jit(solution)/shard_map/all_gather | solution.py:110
  670.3 1.9 broadcast_in_dim.16
  672.2 67.8 %while.13 = (s32[]{:T(128)}, f32[8,272,272]{2,1,0:T(8,128)}, s32[7,3]{0,1:T(4,128)S(1)}, f32[7,8,16,16]{3,2,1,0:T(8,128)S(1)}, s32[]{:T(128)}, /*index=5*/s32[]{:T(128)}, s32[]{:T(128)}) while((s32[]{:T(128)}, f32[8,272,272]{2,1,0:T(8,128)}, s32[7,3]{0,1:T(4,128)S(1)}, f32[7,8,16,16]{3,2,1,0:T(8,128)S(1)}, s32[]{:T(128)}, ...), condition=%wide.region_5.6_spmd, body=%wide.region_4.5_spmd.sunk | while | flops 2056 | bytes 41141 | solution.py:124
  676.6 1.0 bitcast_add_fusion.2
  677.7 4.3 dynamic_update_slice.8
  686.3 1.0 bitcast_add_fusion.2
  687.4 4.3 dynamic_update_slice.8
  697.1 4.2 dynamic_update_slice.8
  705.6 1.0 bitcast_add_fusion.2
  706.7 4.3 dynamic_update_slice.8
  716.4 4.3 dynamic_update_slice.8
  726.1 4.3 dynamic_update_slice.8
  735.8 4.3 dynamic_update_slice.8
  741.0 2.3 pad_add_fusion
  744.2 1.8 fusion.3
  745.9 33.3 %reduce-scatter.2.cloned.1.call-done = f32[8,32,256]{2,1,0:T(8,128)} async-done(((f32[8,256,256]{2,1,0:T(8,128)}), f32[8,32,256]{2,1,0:T(8,128)}) %reduce-scatter.2.cloned.1.call-update) | async-done | bytes 262160 | tf_op jit(solution)/shard_map/reduce_scatter | solution.py:128
  (74 shorter events, 15.9 us)
Async XLA Ops:
  7.2 105.8 %copy-start = (f32[128,16,256]{2,1,0:T(8,128)S(1)}, f32[128,16,256]{2,1,0:T(8,128)}, u32[]{:S(2)}) copy-start(f32[128,16,256]{2,1,0:T(8,128)} %param.12) | copy-start | bytes 6291460
  7.2 6.8 copy-start.6
  15.4 14.9 %copy-start.11 = (s32[64,3]{0,1:T(4,128)S(1)}, s32[64,3]{0,1:T(4,128)}, u32[]{:S(2)}) copy-start(s32[64,3]{0,1:T(4,128)} %param.13) | copy-start | bytes 2308
  15.4 15.0 %copy-start.9 = (s32[1,7]{1,0:T(1,128)S(1)}, s32[1,7]{1,0:T(1,128)}, u32[]{:S(2)}) copy-start(s32[1,7]{1,0:T(1,128)} %param.14) | copy-start | bytes 88
  18.4 12.8 %copy-start.8 = (s32[22016]{0:T(1024)S(1)}, s32[22016]{0:T(1024)}, u32[]{:S(2)}) copy-start(s32[22016]{0:T(1024)} %param.10) | copy-start | bytes 264196
  18.4 99.8 %all-to-all-start = ((f32[2,1,256,688]{3,1,0,2:T(1,128)}), f32[2,1,256,688]{3,1,0,2:T(1,128)}, u32[]{:S(2)}, u32[]{:S(2)}) async-start(f32[2,1,256,688]{3,1,0,2:T(1,128)} %copy.39), calls=%async_computation | async-start | bytes 3145728 | tf_op jit(solution)/shard_map/all_to_all | solution.py:84
  30.3 521.3 %all-reduce.8.cloned.1.call-start = ((), (), s32[]{:S(2)}) async-start(), calls=%async_computation.4 | async-start | bytes 262144
  299.1 4.6 copy-start.5
  307.5 2.4 copy-start.1
  309.8 1.3 copy-start.3
  397.2 9.8 %copy-start.10 = (s32[128]{0:T(128)S(1)}, s32[128]{0:T(128)}, u32[]{:S(2)}) copy-start(s32[128]{0:T(128)} %param.15) | copy-start | bytes 1540
  397.2 11.4 %copy-start.12 = (u32[256]{0:T(256)S(1)}, u32[256]{0:T(256)}, u32[]{:S(2)}) copy-start(u32[256]{0:T(256)} %constant.145) | copy-start | bytes 3076
  407.9 210.2 %all-reduce.6.cloned.1.call-start = ((), (), s32[]{:S(2)}) async-start(), calls=%async_computation.2 | async-start | bytes 524288 | tf_op jit(solution)/shard_map/psum | solution.py:100
  553.6 225.6 %reduce-scatter.2.cloned.1.call-start = ((), (), s32[]{:S(2)}) async-start(), calls=%async_computation.3 | async-start | bytes 2359296 | tf_op jit(solution)/shard_map/reduce_scatter | solution.py:128
  741.0 2.5 copy-start.2
  741.0 3.2 copy-start.4
  744.2 35.1 %copy-start.7 = (f32[4,128,128]{2,1,0:T(8,128)S(1)}, f32[4,128,128]{2,1,0:T(8,128)}, u32[]{:S(2)}) copy-start(f32[4,128,128]{2,1,0:T(8,128)} %all-reduce.6.cloned.1.call-done) | copy-start | bytes 786436
Sparse Core Ops, SparseCore 0:
  408.0 143.4 all-reduce.7
  554.5 63.6 all-reduce.5
  746.1 33.1 reduce-scatter.1
where the time goes:
time: 800 us; the launch traced here: 787 us
  local copies, waits for them, and re-layouts  383 us (48%)
  waiting for transfers between devices  239 us (30%)
  blocking collectives  49.4 us (6%)
  matrix products  46 us (6%)
  loops' own time  26.6 us (3%)
  between operations  15.7 us (2%)
  other arithmetic  14.8 us (2%)
  starting transfers between devices  12 us (2%)
    unnamed x4, waiting for transfers between devices  142 us
    gather x1, local copies, waits for them, and re-layouts, on_device(): spectra = received[:, :, :, slot_map].reshape(2, bands_here, planes, KG, KG)  119 us
    scatter x1, local copies, waits for them, and re-layouts, column_slots(): filled = jnp.zeros((total + 1,), jnp.int32).at[target].set(jnp.arange(sti...  81.4 us
    concatenate x1, local copies, waits for them, and re-layouts, wrap_pad(): return jnp.concatenate([field, field[..., :BOX]], axis=-1)  75.1 us
    psum x1, waiting for transfers between devices, on_device(): atom_totals = lax.psum(partial_matrices, 'band')  64 us
    all_gather x1, blocking collectives, on_device(): every_box = lax.all_gather(box_part, 'grid', axis=0, tiled=True)  49.4 us
    reduce_scatter x1, waiting for transfers between devices, on_device(): result = lax.psum_scatter(total, 'band', scatter_dimension=1, tiled=True)  33.3 us
    dynamic_update_slice x7, local copies, waits for them, and re-layouts, place(): return lax.dynamic_update_slice(acc, current + pieces[index], corner)  29.9 us
  transfers between devices with their start and end apart: 4, of which 3 were waited for; matrix products, arithmetic and copies ran while one was open for 11% of the time, Pallas kernels for 0%

commit v1 on v0

--- a/solution.py
+++ b/solution.py
@@ -107,7 +107,9 @@
     layers_here = layers_here.reshape(NFUNC, thickness * BOX * BOX)
     halfway = jnp.einsum("sij,jc->sic", atom_totals, layers_here, precision=HIGH)
     box_part = jnp.sum(halfway * layers_here[None], axis=1)
-    every_box = lax.all_gather(box_part, "grid", axis=0, tiled=True)
+    every_box = jnp.concatenate(
+        lax.all_to_all(jnp.stack([box_part] * lax.axis_size("grid")), "grid", 0, 0), axis=0
+    )
     mine = jnp.dot(slot_pick, every_box, precision=HIGH).reshape(listed_count, thickness, BOX * BOX)
 
     def box_piece(offsets, box_rows):

time: 800 us -> 773 us (0.966)
  blocking collectives: 49.4 us -> 0 us
  starting transfers between devices: 12 us -> 22.2 us
  waiting for transfers between devices: 239 us -> 249 us
    all_gather x1 -> x0, blocking collectives: 49.4 us -> none  [on_device(): every_box = lax.all_gather(box_part, 'grid', axis=0, tiled=True)]
    all_to_all x0 -> x1, starting transfers between devices: none -> 10.2 us  [on_device(): lax.all_to_all(jnp.stack([box_part] * lax.axis_size('grid')), 'grid', 0, 0)]
    all_to_all x0 -> x1, waiting for transfers between devices: none -> 9.58 us  [on_device(): lax.all_to_all(jnp.stack([box_part] * lax.axis_size('grid')), 'grid', 0, 0)]
  transfers between devices with their start and end apart: 4 -> 5, of which waited for: 3 -> 4; matrix products, arithmetic and copies ran while one was open for 11% -> 12% of each run, Pallas kernels for 0% -> 0%
where the time goes in v1:
time: 773 us; the launch traced here: 760 us
  local copies, waits for them, and re-layouts  384 us (50%)
  waiting for transfers between devices  249 us (32%)
  matrix products  46.1 us (6%)
  loops' own time  28.1 us (4%)
  starting transfers between devices  22.2 us (3%)
  between operations  15.7 us (2%)
  other arithmetic  14.8 us (2%)
    unnamed x4, waiting for transfers between devices  142 us
    gather x1, local copies, waits for them, and re-layouts, on_device(): spectra = received[:, :, :, slot_map].reshape(2, bands_here, planes, KG, KG)  119 us
    scatter x1, local copies, waits for them, and re-layouts, column_slots(): filled = jnp.zeros((total + 1,), jnp.int32).at[target].set(jnp.arange(sti...  81.4 us
    concatenate x1, local copies, waits for them, and re-layouts, wrap_pad(): return jnp.concatenate([field, field[..., :BOX]], axis=-1)  74.9 us
    psum x1, waiting for transfers between devices, on_device(): atom_totals = lax.psum(partial_matrices, 'band')  64.1 us
    reduce_scatter x1, waiting for transfers between devices, on_device(): result = lax.psum_scatter(total, 'band', scatter_dimension=1, tiled=True)  33.1 us
    dynamic_update_slice x7, local copies, waits for them, and re-layouts, place(): return lax.dynamic_update_slice(acc, current + pieces[index], corner)  29.9 us
    another operation x1, loops' own time, on_device(): lax.fori_loop(0, listed_count, place, jnp.zeros((planes, GRID + BOX, GRID...  28.1 us
  transfers between devices with their start and end apart: 5, of which 4 were waited for; matrix products, arithmetic and copies ran while one was open for 12% of the time, Pallas kernels for 0%

profile of v1, /device:TPU:8, one launch (start us, length us, event | category | flops | bytes accessed | tf_op | source)
XLA Modules:
  0.0 759.6 jit_solution(1231596197057272579)
XLA Ops:
  7.2 2.4 fusion.16
  9.6 2.2 fusion.18
  11.8 2.2 fusion.8
  14.0 1.2 fusion.9
  15.4 3.0 copy.61
  18.4 11.9 %all-to-all-start = ((f32[2,1,256,688]{3,1,0,2:T(1,128)}), f32[2,1,256,688]{3,1,0,2:T(1,128)}, u32[]{:S(2)}, u32[]{:S(2)}) async-start(f32[2,1,256,688]{3,1,0,2:T(1,128)} %copy.61), calls=%async_computation | async-start | bytes 3145728 | tf_op jit(solution)/shard_map/all_to_all | solution.py:84
  31.3 81.4 %scatter_custom_fusion = s32[16385]{0:T(1024)S(1)} fusion(s32[22016]{0:T(1024)S(1)} %compare_select_fusion, s32[22016]{0:T(1024)S(1)} %iota.50, s32[]{:T(128)} %constant.80.clone.1), kind=kCustom, calls=%fused_computation.75 | custom fusion | bytes 65544 | tf_op jit(solution)/shard_map/scatter | solution.py:38
  113.0 5.2 convolution_bitcast_fusion
  118.1 2.7 copy.113
  120.8 21.8 %copy.91 = f32[2,1,8,32,688]{2,0,4,3,1:T(2,128)} copy(f32[2,1,8,32,688]{4,2,3,0,1:T(8,128)} %bitcast.134) | data formatting | bytes 2818048 | tf_op jit(solution)/shard_map/all_to_all | solution.py:84
  142.7 118.8 %gather_fusion = f32[16384,2,8]{2,1,0:T(2,128)} fusion(f32[2,8,22016]{1,0,2:T(2,128)} %bitcast.132, s32[16384]{0:T(1024)S(1)} %fusion.42), kind=kCustom, calls=%fused_computation | custom fusion | bytes 2162688 | tf_op jit(solution)/shard_map/gather | solution.py:86
  261.5 19.3 %fusion.135 = (f32[1,8,16384]{1,0,2:T(1,128)}, f32[1,8,16384]{1,0,2:T(1,128)}) fusion(f32[2,8,16384]{1,0,2:T(2,128)} %bitcast.133), kind=kLoop, calls=%fused_computation.180 | loop fusion | bytes 2097152 | tf_op jit(solution)/shard_map/slice | solution.py:87
  280.8 5.1 copy.92
  285.9 2.5 fusion.34
  288.4 2.4 fusion.27
  290.9 5.3 copy.94
  296.2 2.7 convolution_subtract_fusion.1
  298.9 2.3 fusion.37
  301.2 2.3 fusion.29
  303.5 1.5 convolution_add_fusion.1
  305.0 2.3 convolution_subtract_fusion
  307.3 2.3 convolution_add_fusion
  309.7 1.3 copy-done.3
  311.0 3.0 fusion.2
  314.0 74.9 %copy.75 = f32[2,1,8,272,272]{2,0,1,4,3:T(2,128)} copy(f32[2,1,8,272,272]{4,3,2,1,0:T(8,128)} %fusion.2) | data formatting | bytes 9469952 | tf_op jit(solution)/shard_map/concatenate | solution.py:51
  388.9 5.3 gather_fusion.2
  394.2 2.6 copy.76
  396.8 9.8 %fusion.11 = f32[1,7,2,128]{3,2,1,0:T(2,128)S(1)} fusion(f32[7,2,8,256]{3,1,2,0:T(2,128)S(1)} %copy.76, f32[7,128,8,256]{3,2,1,0:T(8,128)} %convolution_bitcast_fusion), kind=kOutput, calls=%fused_computation.34 | convolution fusion | flops 44040192 | bytes 7461888 | tf_op jit(solution)/shard_map/vmap(ipc,xbpc->bxi)/dot_general | solution.py:82
  409.5 141.7 %all-reduce.8.cloned.1.call-done = f32[128,256]{1,0:T(8,128)} async-done(((f32[128,256]{1,0:T(8,128)}), f32[128,256]{1,0:T(8,128)}) %all-reduce.8.cloned.1.call-update) | async-done | bytes 131088
  551.9 1.3 fusion.57
  553.7 64.1 %all-reduce.6.cloned.1.call-done = f32[4,128,128]{2,1,0:T(8,128)} async-done(((f32[4,128,128]{2,1,0:T(8,128)}), f32[4,128,128]{2,1,0:T(8,128)}) %all-reduce.6.cloned.1.call-update) | async-done | bytes 262160 | tf_op jit(solution)/shard_map/psum | solution.py:100
  617.8 2.0 fusion.10
  620.5 10.2 %all-to-all-start.1 = ((f32[32,4,512]{2,1,0:T(4,128)}), f32[32,4,512]{2,1,0:T(4,128)S(1)}, u32[]{:S(2)}, u32[]{:S(2)}) async-start(f32[32,4,512]{2,1,0:T(4,128)} %stack.20), calls=%async_computation.1 | async-start | bytes 524288 | tf_op jit(solution)/shard_map/all_to_all | solution.py:111
  630.8 9.6 %all-to-all-done.1 = f32[32,4,512]{2,1,0:T(4,128)S(1)} async-done(((f32[32,4,512]{2,1,0:T(4,128)}), f32[32,4,512]{2,1,0:T(4,128)S(1)}, u32[]{:S(2)}, u32[]{:S(2)}) %all-to-all-start.1) | async-done | bytes 262176 | tf_op jit(solution)/shard_map/all_to_all | solution.py:111
  641.3 1.9 broadcast_in_dim.16
  643.3 69.9 %while.13 = (s32[]{:T(128)}, f32[8,272,272]{2,1,0:T(8,128)}, s32[7,3]{0,1:T(4,128)S(1)}, f32[7,8,16,16]{3,2,1,0:T(8,128)S(1)}, s32[]{:T(128)}, /*index=5*/s32[]{:T(128)}, s32[]{:T(128)}) while((s32[]{:T(128)}, f32[8,272,272]{2,1,0:T(8,128)}, s32[7,3]{0,1:T(4,128)S(1)}, f32[7,8,16,16]{3,2,1,0:T(8,128)S(1)}, s32[]{:T(128)}, ...), condition=%wide.region_5.6_spmd, body=%wide.region_4.5_spmd.sunk | while | flops 2056 | bytes 41141 | solution.py:126
  647.9 1.0 bitcast_add_fusion.2
  649.0 4.3 dynamic_update_slice.8
  659.0 4.3 dynamic_update_slice.8
  668.9 4.2 dynamic_update_slice.8
  678.8 4.3 dynamic_update_slice.8
  688.8 4.3 dynamic_update_slice.8
  697.8 1.0 bitcast_add_fusion.2
  698.8 4.3 dynamic_update_slice.8
  708.8 4.3 dynamic_update_slice.8
  714.1 2.3 pad_add_fusion
  717.2 1.8 fusion.3
  719.0 33.1 %reduce-scatter.2.cloned.1.call-done = f32[8,32,256]{2,1,0:T(8,128)} async-done(((f32[8,256,256]{2,1,0:T(8,128)}), f32[8,32,256]{2,1,0:T(8,128)}) %reduce-scatter.2.cloned.1.call-update) | async-done | bytes 262160 | tf_op jit(solution)/shard_map/reduce_scatter | solution.py:130
  (76 shorter events, 18.3 us)
Async XLA Ops:
  7.2 105.8 %copy-start = (f32[128,16,256]{2,1,0:T(8,128)S(1)}, f32[128,16,256]{2,1,0:T(8,128)}, u32[]{:S(2)}) copy-start(f32[128,16,256]{2,1,0:T(8,128)} %param.12) | copy-start | bytes 6291460
  7.2 6.8 copy-start.6
  15.4 14.9 %copy-start.11 = (s32[64,3]{0,1:T(4,128)S(1)}, s32[64,3]{0,1:T(4,128)}, u32[]{:S(2)}) copy-start(s32[64,3]{0,1:T(4,128)} %param.13) | copy-start | bytes 2308
  15.4 15.0 %copy-start.9 = (s32[1,7]{1,0:T(1,128)S(1)}, s32[1,7]{1,0:T(1,128)}, u32[]{:S(2)}) copy-start(s32[1,7]{1,0:T(1,128)} %param.14) | copy-start | bytes 88
  18.4 12.8 %copy-start.8 = (s32[22016]{0:T(1024)S(1)}, s32[22016]{0:T(1024)}, u32[]{:S(2)}) copy-start(s32[22016]{0:T(1024)} %param.10) | copy-start | bytes 264196
  18.4 99.8 %all-to-all-start = ((f32[2,1,256,688]{3,1,0,2:T(1,128)}), f32[2,1,256,688]{3,1,0,2:T(1,128)}, u32[]{:S(2)}, u32[]{:S(2)}) async-start(f32[2,1,256,688]{3,1,0,2:T(1,128)} %copy.61), calls=%async_computation | async-start | bytes 3145728 | tf_op jit(solution)/shard_map/all_to_all | solution.py:84
  30.3 520.9 %all-reduce.8.cloned.1.call-start = ((), (), s32[]{:S(2)}) async-start(), calls=%async_computation.5 | async-start | bytes 262144
  298.9 4.6 copy-start.5
  307.3 2.4 copy-start.1
  309.7 1.3 copy-start.3
  396.8 9.8 %copy-start.10 = (s32[128]{0:T(128)S(1)}, s32[128]{0:T(128)}, u32[]{:S(2)}) copy-start(s32[128]{0:T(128)} %param.15) | copy-start | bytes 1540
  396.8 11.4 %copy-start.12 = (u32[256]{0:T(256)S(1)}, u32[256]{0:T(256)}, u32[]{:S(2)}) copy-start(u32[256]{0:T(256)} %constant.145) | copy-start | bytes 3076
  407.6 210.2 %all-reduce.6.cloned.1.call-start = ((), (), s32[]{:S(2)}) async-start(), calls=%async_computation.3 | async-start | bytes 524288 | tf_op jit(solution)/shard_map/psum | solution.py:100
  620.5 19.9 %all-to-all-start.1 = ((f32[32,4,512]{2,1,0:T(4,128)}), f32[32,4,512]{2,1,0:T(4,128)S(1)}, u32[]{:S(2)}, u32[]{:S(2)}) async-start(f32[32,4,512]{2,1,0:T(4,128)} %stack.20), calls=%async_computation.1 | async-start | bytes 524288 | tf_op jit(solution)/shard_map/all_to_all | solution.py:111
  630.7 121.5 %reduce-scatter.2.cloned.1.call-start = ((), (), s32[]{:S(2)}) async-start(), calls=%async_computation.4 | async-start | bytes 2359296 | tf_op jit(solution)/shard_map/reduce_scatter | solution.py:130
  714.1 2.5 copy-start.2
  714.1 3.2 copy-start.4
  717.2 34.9 %copy-start.7 = (f32[4,128,128]{2,1,0:T(8,128)S(1)}, f32[4,128,128]{2,1,0:T(8,128)}, u32[]{:S(2)}) copy-start(f32[4,128,128]{2,1,0:T(8,128)} %all-reduce.6.cloned.1.call-done) | copy-start | bytes 786436
Sparse Core Ops, SparseCore 0:
  407.7 143.4 all-reduce.7
  554.1 63.6 all-reduce.5
  719.2 32.9 reduce-scatter.1
